TPU v7x, 256 devices: a whole 4x4x8 slice. The times are simulated.
256 devices in a mesh: energy: 128 (over y_lo, x, z, core), mode: 2 (over y_hi).
Axes of the slice: x: 4, y: 4 (y_hi: 2, y_lo: 2; y = y_hi * 2 + y_lo), z: 8, core: 2. Of those that a mesh axis runs over, the one named last changes fastest.
Arguments:
- spectral: float32 [128, 896, 896], P('energy', 'mode'), may hold values from -6 to 6
- coupling: bfloat16 [2, 896, 896], P('mode'), may hold values from -0.1875 to 0.1875
- offsets: int32 [2], P('mode'), may hold values from 1 to 2, as said below
- occupation: int32 [2, 128], P('mode', 'energy'), may hold values from 0 to 3
Outputs:
- self_energy: float32 [128, 896, 896], P('energy', 'mode')
Inputs may be any that keep to these rules, and one draw needn't show every extreme that they name: `offsets`: each offset from 1 to 2 belongs to exactly 1 modes.
All inputs are finite; a program needn't handle non-finite values.
Results may differ from a plain program's by a relative error of at most 0.0041.
Values sent between devices are 32-bit elements; how exact they have to be, the bound alone decides.
A program may use at most 64 MiB of HBM per device.

v0:
```python
import jax
import jax.numpy as jnp
from jax import lax
from jax.sharding import PartitionSpec as P

KMAX = 2


def passed_along(value, axis, steps):
    count = lax.axis_size(axis)
    first, last = (max(0, -steps), min(count, count - steps))
    return lax.ppermute(value, axis, [(source, source + steps) for source in range(first, last)])


def split_up(value, dim, devices):
    shape = value.shape
    parts = value.reshape(*shape[:dim], devices, shape[dim] // devices, *shape[dim + 1 :])
    return jnp.moveaxis(parts, dim, 0)


def summed_on_arrival(value, axis, dim):
    parts = split_up(value, dim, lax.axis_size(axis))
    arrived = lax.all_to_all(parts, axis, split_axis=0, concat_axis=0, tiled=True)
    return arrived.sum(axis=0)


def collect_rim(own_block, max_offset):
    per_device = own_block.shape[0]
    farthest = -(-max_offset // per_device)
    requests = []
    for distance in range(farthest, 0, -1):
        requests.append((distance, max(0, distance * per_device - max_offset), per_device))
    for distance in range(1, farthest + 1):
        requests.append((-distance, 0, min(per_device, max_offset - (distance - 1) * per_device)))
    lower_parts = []
    upper_parts = []
    for shift_by, first_row, last_row in requests:
        arrived = passed_along(own_block, "energy", shift_by)
        if shift_by > 0:
            lower_parts.append(arrived)
        else:
            upper_parts.append(arrived)
    return jnp.concatenate(lower_parts + [own_block] + upper_parts, axis=0)


def shards(spectral, coupling, offsets, occupation):
    max_offset = KMAX
    full_block = lax.all_gather(spectral, "mode", axis=1, tiled=True)
    window = collect_rim(full_block, max_offset)
    per_device = spectral.shape[0]
    window_len = window.shape[0]
    position = lax.broadcasted_iota(jnp.int32, (1, per_device, window_len), 2)
    energy_pos = lax.broadcasted_iota(jnp.int32, (1, per_device, window_len), 1) + max_offset
    offset_col = offsets[:, None, None]
    emission = (occupation + 1).astype(jnp.float32)[:, :, None]
    absorption = occupation.astype(jnp.float32)[:, :, None]
    weights_table = jnp.where(position == energy_pos - offset_col, emission, 0.0)
    weights_table = weights_table + jnp.where(position == energy_pos + offset_col, absorption, 0.0)
    combined = jnp.einsum(
        "mew,wij->meij", weights_table, window, precision=lax.Precision.HIGHEST
    ).astype(jnp.bfloat16)
    coupled = jnp.einsum(
        "mij,mejk->meik", coupling, combined, preferred_element_type=jnp.float32
    ).astype(jnp.bfloat16)
    partial_sum = jnp.einsum("meik,mlk->eil", coupled, coupling, preferred_element_type=jnp.float32)
    modes_all = coupling.shape[0] * lax.axis_size("mode")
    summed = summed_on_arrival(partial_sum, "mode", 1)
    return summed / modes_all


def solution(mesh):
    return jax.shard_map(
        shards,
        mesh=mesh,
        in_specs=(P("energy", "mode", None), P("mode", None, None), P("mode"), P("mode", "energy")),
        out_specs=P("energy", "mode", None),
        check_vma=False,
    )
```

profile of v0, /device:TPU:8, one launch (start us, length us, event | category | flops | bytes accessed | tf_op | source)
XLA Modules:
  0.0 262.4 jit_solution(1662050244572922762)
XLA Ops:
  6.5 0.0 copy-start
  6.5 0.0 all-gather.2.cloned.1.call-start
  6.5 0.7 all-gather.2.cloned.1.call-update
  7.3 56.2 %all-gather.2.cloned.1.call-done = f32[1,896,896]{2,1,0:T(8,128)} async-done(((f32[1,448,896]{2,1,0:T(8,128)}), f32[1,896,896]{2,1,0:T(8,128)}) %all-gather.2.cloned.1.call-update) | async-done | bytes 3211280 | tf_op jit(solution)/shard_map/all_gather | solution.py:48
  63.5 3.4 %collective-permute-start = (f32[1,896,896]{2,1,0:T(8,128)}, f32[1,896,896]{2,1,0:T(8,128)S(1)}, u32[]{:S(2)}, u32[]{:S(2)}) collective-permute-start(f32[1,896,896]{2,1,0:T(8,128)} %all-gather.2.cloned.1.call-done), channel_id=1, source_target_pairs={{0,4},{2,6},{4,8},{6,10},{8,12},{10,14},{12,16},{14,18},{16,20},{1... | collective-permute-start | bytes 9633800 | tf_op jit(solution)/shard_map/ppermute | solution.py:12
  66.9 1.9 collective-permute-start.1
  68.8 7.9 %collective-permute-start.2 = (f32[1,896,896]{2,1,0:T(8,128)}, f32[1,896,896]{2,1,0:T(8,128)S(1)}, u32[]{:S(2)}, u32[]{:S(2)}) collective-permute-start(f32[1,896,896]{2,1,0:T(8,128)} %all-gather.2.cloned.1.call-done), channel_id=1, source_target_pairs={{2,0},{4,2},{6,4},{8,6},{10,8},{12,10},{14,12},{16,14},{18,16},{20... | collective-permute-start | bytes 9633800 | tf_op jit(solution)/shard_map/ppermute | solution.py:12
  76.7 2.5 collective-permute-start.3
  80.5 61.7 %collective-permute-done = f32[1,896,896]{2,1,0:T(8,128)S(1)} collective-permute-done((f32[1,896,896]{2,1,0:T(8,128)}, f32[1,896,896]{2,1,0:T(8,128)S(1)}, u32[]{:S(2)}, u32[]{:S(2)}) %collective-permute-start) | collective-permute-done | bytes 3211296 | tf_op jit(solution)/shard_map/ppermute | solution.py:12
  142.2 0.2 constant_dynamic-update-slice_fusion.4
  142.4 0.0 copy-start.1
  142.4 33.4 %collective-permute-done.1 = f32[1,896,896]{2,1,0:T(8,128)S(1)} collective-permute-done((f32[1,896,896]{2,1,0:T(8,128)}, f32[1,896,896]{2,1,0:T(8,128)S(1)}, u32[]{:S(2)}, u32[]{:S(2)}) %collective-permute-start.1) | collective-permute-done | bytes 3211296 | tf_op jit(solution)/shard_map/ppermute | solution.py:12
  175.8 0.2 constant_dynamic-update-slice_fusion.3
  176.0 0.0 copy-done.1
  176.0 0.2 constant_dynamic-update-slice_fusion.2
  176.2 0.0 collective-permute-done.2
  176.2 0.2 constant_dynamic-update-slice_fusion.1
  176.5 4.9 %collective-permute-done.3 = f32[1,896,896]{2,1,0:T(8,128)S(1)} collective-permute-done((f32[1,896,896]{2,1,0:T(8,128)}, f32[1,896,896]{2,1,0:T(8,128)S(1)}, u32[]{:S(2)}, u32[]{:S(2)}) %collective-permute-start.3) | collective-permute-done | bytes 3211296 | tf_op jit(solution)/shard_map/ppermute | solution.py:12
  181.3 0.2 constant_dynamic-update-slice_fusion
  181.5 34.3 %fusion = bf16[1,896,896]{2,0,1:T(2,128)(2,1)S(1)} fusion(f32[5,896,896]{2,1,0:T(8,128)S(1)} %constant_dynamic-update-slice_fusion, f32[]{:T(128)} %bitcast.3, s32[]{:T(128)} %bitcast.2, f32[]{:T(128)} %bitcast.1, s32[]{:T(128)} %bitcast), kind=kOutput, calls=%fused_computation | convolution fusion | flops 48168984 | bytes 17661968 | tf_op jit(solution)/shard_map/mew,wij->meij/dot_general | solution.py:59
  215.8 0.0 copy-done
  215.8 2.0 convolution_convert_fusion
  217.9 2.0 convolution_bitcast_fusion
  219.9 32.2 %all_to_all.5 = f32[2,1,448,896]{3,2,1,0:T(8,128)} all-to-all(f32[2,1,448,896]{3,2,1,0:T(8,128)S(1)} %convolution_bitcast_fusion), channel_id=1, replica_groups=mesh['energy'=128,'mode'=2] {'mode'}, dimensions={0} | all-to-all | bytes 6422528 | tf_op jit(solution)/shard_map/all_to_all | solution.py:23
  252.0 2.3 reduce_sum.9
  254.3 1.3 multiply_bitcast_fusion
Async XLA Ops:
  6.5 209.3 %copy-start = (bf16[1,896,896]{2,1,0:T(8,128)(2,1)S(1)}, bf16[1,896,896]{2,1,0:T(8,128)(2,1)}, u32[]{:S(2)}) copy-start(bf16[1,896,896]{2,1,0:T(8,128)(2,1)} %param.5) | copy-start | bytes 4816900
  6.5 56.9 %all-gather.2.cloned.1.call-start = ((), (), s32[]{:S(2)}) async-start(), calls=%async_computation.1 | async-start | bytes 4816896 | tf_op jit(solution)/shard_map/all_gather | solution.py:48
  63.5 78.7 %collective-permute-start = (f32[1,896,896]{2,1,0:T(8,128)}, f32[1,896,896]{2,1,0:T(8,128)S(1)}, u32[]{:S(2)}, u32[]{:S(2)}) collective-permute-start(f32[1,896,896]{2,1,0:T(8,128)} %all-gather.2.cloned.1.call-done), channel_id=1, source_target_pairs={{0,4},{2,6},{4,8},{6,10},{8,12},{10,14},{12,16},{14,18},{16,20},{1... | collective-permute-start | bytes 9633800 | tf_op jit(solution)/shard_map/ppermute | solution.py:12
  66.9 108.9 %collective-permute-start.1 = (f32[1,896,896]{2,1,0:T(8,128)}, f32[1,896,896]{2,1,0:T(8,128)S(1)}, u32[]{:S(2)}, u32[]{:S(2)}) collective-permute-start(f32[1,896,896]{2,1,0:T(8,128)} %all-gather.2.cloned.1.call-done), channel_id=1, source_target_pairs={{0,2},{2,4},{4,6},{6,8},{8,10},{10,12},{12,14},{14,16},{16,18},{18... | collective-permute-start | bytes 9633800 | tf_op jit(solution)/shard_map/ppermute | solution.py:12
  68.8 107.4 %collective-permute-start.2 = (f32[1,896,896]{2,1,0:T(8,128)}, f32[1,896,896]{2,1,0:T(8,128)S(1)}, u32[]{:S(2)}, u32[]{:S(2)}) collective-permute-start(f32[1,896,896]{2,1,0:T(8,128)} %all-gather.2.cloned.1.call-done), channel_id=1, source_target_pairs={{2,0},{4,2},{6,4},{8,6},{10,8},{12,10},{14,12},{16,14},{18,16},{20... | collective-permute-start | bytes 9633800 | tf_op jit(solution)/shard_map/ppermute | solution.py:12
  76.7 104.6 %collective-permute-start.3 = (f32[1,896,896]{2,1,0:T(8,128)}, f32[1,896,896]{2,1,0:T(8,128)S(1)}, u32[]{:S(2)}, u32[]{:S(2)}) collective-permute-start(f32[1,896,896]{2,1,0:T(8,128)} %all-gather.2.cloned.1.call-done), channel_id=1, source_target_pairs={{4,0},{6,2},{8,4},{10,6},{12,8},{14,10},{16,12},{18,14},{20,16},{2... | collective-permute-start | bytes 9633800 | tf_op jit(solution)/shard_map/ppermute | solution.py:12
  142.4 33.6 %copy-start.1 = (f32[1,896,896]{2,1,0:T(8,128)S(1)}, f32[1,896,896]{2,1,0:T(8,128)}, u32[]{:S(2)}) copy-start(f32[1,896,896]{2,1,0:T(8,128)} %all-gather.2.cloned.1.call-done) | copy-start | bytes 9633796
Sparse Core Ops, SparseCore 0:
  9.2 54.2 all-gather.1
where the time goes:
time: 264 us; the launch traced here: 262 us
  waiting for transfers between devices  157 us (59%)
  matrix products  38.3 us (15%)
  blocking collectives  32.2 us (12%)
  starting transfers between devices  15.7 us (6%)
  between operations  14.8 us (6%)
  other arithmetic  3.54 us (1%)
    ppermute x4, waiting for transfers between devices, passed_along(): lax.ppermute(value, axis, [(source, source + steps) for source in range(f...  100 us
    all_gather x1, waiting for transfers between devices, shards(): full_block = lax.all_gather(spectral, 'mode', axis=1, tiled=True)  56.2 us
    dot_general x1, matrix products, shards(): jnp.einsum('mew,wij->meij', weights_table, window, precision=lax.Precisio...  34.3 us
    all_to_all x1, blocking collectives, summed_on_arrival(): lax.all_to_all(parts, axis, split_axis=0, concat_axis=0, tiled=True)  32.2 us
    ppermute x4, starting transfers between devices, passed_along(): lax.ppermute(value, axis, [(source, source + steps) for source in range(f...  15.7 us
  transfers between devices with their start and end apart: 5, of which 4 were waited for; matrix products, arithmetic and copies ran while one was open for 0% of the time, Pallas kernels for 0%

commit v1 on v0

v1 whole, which is shorter than its diff:
```python
import functools

import jax
import jax.numpy as jnp
from jax import lax
from jax.experimental import pallas as pl
from jax.experimental.pallas import tpu as pltpu
from jax.sharding import PartitionSpec as P

MESH = pl.DeviceIdType.MESH
CORES, ALONG_Z, ALONG_X = 2, 8, 4
CHUNK = 64
F32, BF16 = jnp.float32, jnp.bfloat16


def dot_nt(a, b):
    return lax.dot_general(a, b, (((1,), (1,)), ((), ())), preferred_element_type=F32)


def dot_nn(a, b):
    return jnp.dot(a, b, preferred_element_type=F32)


def kernel(
    energies,
    x_ref,
    g_ref,
    off_ref,
    occ_ref,
    o_ref,
    near,
    g_mine,
    g_slice,
    g_got,
    g_other,
    cols,
    coupled,
    p_out,
    p_in,
    occ_mine,
    occ_got,
    load_sem,
    near_send,
    near_recv,
    fwd_send,
    fwd_recv,
    sib_send,
    sib_recv,
    g_send,
    g_recv,
    occ_send,
    occ_recv,
    p_send,
    p_recv,
):
    e = lax.axis_index("energy")
    m = lax.axis_index("mode")
    rows, norb = x_ref.shape[1], x_ref.shape[2]
    chunks = rows // CHUNK
    core = e % CORES
    x_at = (e // (CORES * ALONG_Z)) % ALONG_X
    slices = CORES * ALONG_X
    depth = norb // slices
    up = (lax.rem(e + 2, energies), m)
    down = (lax.rem(e + energies - 2, energies), m)
    sibling = (e + 1 - 2 * core, m)
    partner = (e, 1 - m)
    across = (lax.rem(e + energies // 2, energies), 1 - m)
    x_peers = []
    for step in range(1, ALONG_X):
        there = lax.rem(x_at + step, ALONG_X)
        x_peers.append((e + (there - x_at) * (CORES * ALONG_Z), m))

    load = pltpu.make_async_copy(g_ref.at[0], g_mine, load_sem)
    load.start()
    barrier = pltpu.get_barrier_semaphore()
    greeted = [up, down, sibling, partner, across, *x_peers]
    for device in greeted:
        pl.semaphore_signal(barrier, inc=1, device_id=device, device_id_type=MESH)
    pl.semaphore_wait(barrier, len(greeted))

    def remote(src, dst, send, recv, device):
        return pltpu.make_async_remote_copy(
            src_ref=src, dst_ref=dst, send_sem=send, recv_sem=recv, device_id=device, device_id_type=MESH
        )

    def at(i, base=0):
        return pl.ds(pl.multiple_of(base + i * CHUNK, CHUNK), CHUNK)

    def to_up(i):
        return remote(x_ref.at[0, at(i)], near.at[0, at(i)], near_send.at[0, i], near_recv.at[0, i], up)

    def to_down(i):
        return remote(x_ref.at[0, at(i)], near.at[1, at(i)], near_send.at[1, i], near_recv.at[1, i], down)

    def to_sibling(i):
        return remote(near.at[1 - core, at(i)], near.at[3, at(i)], fwd_send.at[i], fwd_recv.at[i], sibling)

    def to_partner(i):
        return remote(p_out.at[at(i)], p_in.at[at(i)], p_send.at[i], p_recv.at[i], partner)

    own_to_sibling = remote(x_ref.at[0], near.at[2], sib_send, sib_recv, sibling)

    @pl.loop(0, chunks)
    def _(i):
        to_up(i).start()
        to_down(i).start()

    own_to_sibling.start()

    my_slice = x_at * CORES + core
    load.wait()
    g_slice[...] = g_mine[pl.ds(pl.multiple_of(my_slice * depth, 16), depth), :].astype(F32)
    occ_mine[...] = jnp.full(occ_mine.shape, occ_ref[0, 0].astype(F32), F32)
    slice_across = remote(g_slice, g_got.at[my_slice], g_send.at[0], g_recv.at[0], across)
    slice_across.start()
    occ_copy = remote(occ_mine, occ_got, occ_send, occ_recv, partner)
    occ_copy.start()

    def own_columns(matrix):
        pick = lax.broadcasted_iota(jnp.int32, (norb, rows), 0) == (
            lax.broadcasted_iota(jnp.int32, (norb, rows), 1) + m * rows
        )
        return dot_nn(matrix, jnp.where(pick, 1.0, 0.0).astype(BF16)).astype(BF16)

    cols[0] = own_columns(g_mine[...])

    slice_across.wait_recv()
    spread = []
    for step in range(1, ALONG_X):
        copy = remote(
            g_got.at[my_slice], g_got.at[my_slice], g_send.at[step], g_recv.at[step], x_peers[step - 1]
        )
        copy.start()
        spread.append(copy)
    to_sib = [remote(g_got.at[my_slice], g_got.at[my_slice], g_send.at[4], g_recv.at[4], sibling)]
    to_sib[0].start()

    occ_copy.wait_recv()
    own_one = off_ref[0] == 1
    own_occ = occ_mine[0:1, 0:1]
    other_occ = occ_got[0:1, 0:1]
    one_sel = jnp.where(own_one, 1.0, 0.0)
    is_one = (one_sel, 1.0 - one_sel)
    low2 = jnp.where(e >= 2, 1.0, 0.0)
    high2 = jnp.where(e < energies - 2, 1.0, 0.0)
    on_core = core.astype(F32)
    third = jnp.where((e > 0) & (e < energies - 1), 1.0, 0.0)
    weights = []
    for occ, one in zip((own_occ, other_occ), is_one):
        weights.append(
            (
                (occ + 1.0) * ((1.0 - one) * low2),
                occ * ((1.0 - one) * high2),
                (occ + on_core) * one,
                (occ + (1.0 - on_core)) * (one * third),
            )
        )

    own_to_sibling.wait_recv()

    def take_chunk(i):
        to_up(i).wait_recv()
        to_down(i).wait_recv()
        to_sibling(i).start()

    def couple(i, which, matrix):
        w = weights[which]
        combined = w[0] * near[0, at(i), :] + w[1] * near[1, at(i), :]
        combined = combined + (w[2] * near[2, at(i), :] + w[3] * near[3, at(i), :])
        coupled[which, at(i), :] = dot_nt(combined.astype(BF16), matrix[...]).astype(BF16)

    @pl.loop(0, chunks - 1)
    def _(i):
        take_chunk(i)
        to_sibling(i).wait_recv()
        couple(i, 0, g_mine)

    for step in range(1, ALONG_X):
        peer_slice = lax.rem(x_at + ALONG_X - step, ALONG_X) * CORES + core
        remote(
            g_got.at[peer_slice], g_got.at[peer_slice], g_send.at[step], g_recv.at[step], x_peers[step - 1]
        ).wait_recv()
        copy = remote(
            g_got.at[peer_slice], g_got.at[peer_slice], g_send.at[4 + step], g_recv.at[4 + step], sibling
        )
        copy.start()
        to_sib.append(copy)
    for step in range(ALONG_X):
        peer_slice = lax.rem(x_at + ALONG_X - step, ALONG_X) * CORES + 1 - core
        remote(
            g_got.at[peer_slice], g_got.at[peer_slice], g_send.at[4 + step], g_recv.at[4 + step], sibling
        ).wait_recv()
    for k in range(slices):
        g_other[k * depth : (k + 1) * depth, :] = g_got[k].astype(BF16)
    cols[1] = own_columns(g_other[...])

    @pl.loop(0, chunks - 1)
    def _(i):
        couple(i, 1, g_other)

    last = chunks - 1
    take_chunk(last)
    to_sibling(last).wait_recv()
    couple(last, 0, g_mine)
    couple(last, 1, g_other)

    def partial(i, base):
        there = at(i, base)
        return dot_nn(cols[0, there, :], coupled[0]) + dot_nn(cols[1, there, :], coupled[1])

    @pl.loop(0, chunks)
    def _(i):
        p_out[at(i), :] = partial(i, (1 - m) * rows)
        to_partner(i).start()

    @pl.loop(0, chunks)
    def _(i):
        o_ref[0, at(i), :] = partial(i, m * rows)

    @pl.loop(0, chunks)
    def _(i):
        to_partner(i).wait_recv()
        o_ref[0, at(i), :] = (o_ref[0, at(i), :] + p_in[at(i), :]) * 0.5

    @pl.loop(0, chunks)
    def _(i):
        to_up(i).wait_send()
        to_down(i).wait_send()
        to_sibling(i).wait_send()
        to_partner(i).wait_send()

    own_to_sibling.wait_send()
    slice_across.wait_send()
    occ_copy.wait_send()
    for copy in spread + to_sib:
        copy.wait_send()


def shards(energies, spectral, coupling, offsets, occupation):
    _, rows, norb = spectral.shape
    chunks = rows // CHUNK
    slices = CORES * ALONG_X
    dma = pltpu.SemaphoreType.DMA
    anywhere = pl.BlockSpec(memory_space=pltpu.HBM)
    scalar = pl.BlockSpec(memory_space=pltpu.SMEM)
    return pl.pallas_call(
        functools.partial(kernel, energies),
        out_shape=jax.ShapeDtypeStruct(spectral.shape, F32),
        in_specs=[anywhere, anywhere, scalar, scalar],
        out_specs=pl.BlockSpec(memory_space=pltpu.VMEM),
        scratch_shapes=[
            pltpu.VMEM((4, rows, norb), F32),
            pltpu.VMEM((norb, norb), BF16),
            pltpu.VMEM((norb // slices, norb), F32),
            pltpu.VMEM((slices, norb // slices, norb), F32),
            pltpu.VMEM((norb, norb), BF16),
            pltpu.VMEM((2, norb, rows), BF16),
            pltpu.VMEM((2, rows, norb), BF16),
            pltpu.VMEM((rows, norb), F32),
            pltpu.VMEM((rows, norb), F32),
            pltpu.VMEM((8, 128), F32),
            pltpu.VMEM((8, 128), F32),
            dma,
            dma((2, chunks)),
            dma((2, chunks)),
            dma((chunks,)),
            dma((chunks,)),
            dma,
            dma,
            dma((8,)),
            dma((8,)),
            dma,
            dma,
            dma((chunks,)),
            dma((chunks,)),
        ],
        compiler_params=pltpu.CompilerParams(
            collective_id=0, has_side_effects=True, vmem_limit_bytes=48 << 20
        ),
        name="born_step",
    )(spectral, coupling, offsets, occupation)


def solution(mesh):
    return jax.shard_map(
        functools.partial(shards, mesh.shape["energy"]),
        mesh=mesh,
        in_specs=(P("energy", "mode", None), P("mode", None, None), P("mode"), P("mode", "energy")),
        out_specs=P("energy", "mode", None),
        check_vma=False,
    )
```

time: 264 us -> 117 us (0.44)
  waiting for transfers between devices: 157 us -> 0 us
  Pallas kernels: 0 us -> 110 us
  matrix products: 38.3 us -> 0 us
  blocking collectives: 32.2 us -> 0 us
  starting transfers between devices: 15.7 us -> 0 us
  between operations: 14.8 us -> 1.31 us
  other arithmetic: 3.54 us -> 0 us
  local copies, waits for them, and re-layouts: 1.05 us -> 3.99 us
    pallas_call x0 -> x1, Pallas kernels: none -> 110 us  [shards(): pl.pallas_call(functools.partial(kernel, energies), out_shape=jax.ShapeDt...]
    ppermute x4 -> x0, waiting for transfers between devices: 100 us -> none  [passed_along(): lax.ppermute(value, axis, [(source, source + steps) for source in range(f...]
    all_gather x1 -> x0, waiting for transfers between devices: 56.2 us -> none  [shards(): full_block = lax.all_gather(spectral, 'mode', axis=1, tiled=True)]
    dot_general x3 -> x0, matrix products: 38.3 us -> none  [the longest x1 34.3 us: shards(): jnp.einsum('mew,wij->meij', weights_table, window, precision=lax.Precisio...]
    all_to_all x1 -> x0, blocking collectives: 32.2 us -> none  [summed_on_arrival(): lax.all_to_all(parts, axis, split_axis=0, concat_axis=0, tiled=True)]
    ppermute x4 -> x0, starting transfers between devices: 15.7 us -> none  [passed_along(): lax.ppermute(value, axis, [(source, source + steps) for source in range(f...]
    unnamed x8 -> x5, local copies, waits for them, and re-layouts: 0.84 us -> 3.99 us
  transfers between devices with their start and end apart: 5 -> 0, of which waited for: 4 -> 0; matrix products, arithmetic and copies ran while one was open for 0% -> 0% of each run, Pallas kernels for 0% -> 0%
where the time goes in v1:
time: 117 us; the launch traced here: 115 us
  Pallas kernels  110 us (94%)
  local copies, waits for them, and re-layouts  3.99 us (3%)
  between operations  1.31 us (1%)
    pallas_call x1, Pallas kernels, shards(): pl.pallas_call(functools.partial(kernel, energies), out_shape=jax.ShapeDt...  110 us
    unnamed x5, local copies, waits for them, and re-layouts  3.99 us

profile of v1, /device:TPU:8, one launch (start us, length us, event | category | flops | bytes accessed | tf_op | source)
XLA Modules:
  0.0 115.1 jit_solution(6065215060592270550)
XLA Ops:
  1.3 0.0 copy-start
  1.3 1.4 %copy-done = f32[1,448,896]{2,1,0:T(8,128)S(1)} copy-done((f32[1,448,896]{2,1,0:T(8,128)S(1)}, f32[1,448,896]{2,1,0:T(8,128)}, u32[]{:S(2)}) %copy-start) | copy-done | bytes 1605656
  2.7 0.0 copy-start.1
  2.7 1.4 %copy-done.1 = bf16[1,896,896]{2,1,0:T(8,128)(2,1)S(1)} copy-done((bf16[1,896,896]{2,1,0:T(8,128)(2,1)S(1)}, bf16[1,896,896]{2,1,0:T(8,128)(2,1)}, u32[]{:S(2)}) %copy-start.1) | copy-done | bytes 1605656
  4.1 109.8 %born_step.1 = f32[1,448,896]{2,1,0:T(8,128)S(1)} custom-call(f32[1,448,896]{2,1,0:T(8,128)S(1)} %copy-done, bf16[1,896,896]{2,1,0:T(8,128)(2,1)S(1)} %copy-done.1, s32[1]{0:T(128)S(6)} %copy.6.off_ref, s32[1,1]{1,0:T(1,128)S(6)} %copy.7.occ_ref), custom_call_target="tpu_custom_call" | custom-call | tf_op jit(solution)/shard_map/born_step/pallas_call | solution.py:247
  114.0 1.2 %copy.8 = f32[1,448,896]{2,1,0:T(8,128)} copy(f32[1,448,896]{2,1,0:T(8,128)S(1)} %born_step.1) | data formatting | bytes 3211264
Async XLA Ops:
  1.3 1.4 %copy-start = (f32[1,448,896]{2,1,0:T(8,128)S(1)}, f32[1,448,896]{2,1,0:T(8,128)}, u32[]{:S(2)}) copy-start(f32[1,448,896]{2,1,0:T(8,128)} %x_ref.1) | copy-start | bytes 4816900
  2.7 1.4 %copy-start.1 = (bf16[1,896,896]{2,1,0:T(8,128)(2,1)S(1)}, bf16[1,896,896]{2,1,0:T(8,128)(2,1)}, u32[]{:S(2)}) copy-start(bf16[1,896,896]{2,1,0:T(8,128)(2,1)} %g_ref.1) | copy-start | bytes 4816900

commit v2 on v1

v2 whole, which is shorter than its diff:
```python
import functools

import jax
import jax.numpy as jnp
from jax import lax
from jax.experimental import pallas as pl
from jax.experimental.pallas import tpu as pltpu
from jax.sharding import PartitionSpec as P

MESH = pl.DeviceIdType.MESH
CORES, ALONG_Z, ALONG_X = 2, 8, 4
CHUNK = 64
LANES = 128
PIECE = 256
F32, BF16 = jnp.float32, jnp.bfloat16


def dot(a, b):
    return jnp.dot(a, b, preferred_element_type=F32)


def kernel(
    energies,
    x_ref,
    g_ref,
    off_ref,
    occ_ref,
    o_ref,
    near,
    g_mine,
    g_send_buf,
    g_got,
    turned,
    cols,
    coupled,
    p_out,
    p_in,
    occ_mine,
    occ_got,
    load_sem,
    near_send,
    near_recv,
    fwd_send,
    fwd_recv,
    sib_send,
    sib_recv,
    g_send,
    g_recv,
    occ_send,
    occ_recv,
    p_send,
    p_recv,
):
    e = lax.axis_index("energy")
    m = lax.axis_index("mode")
    rows, norb = x_ref.shape[1], x_ref.shape[2]
    chunks = rows // CHUNK
    core = e % CORES
    x_at = (e // (CORES * ALONG_Z)) % ALONG_X
    up = (lax.rem(e + 2, energies), m)
    down = (lax.rem(e + energies - 2, energies), m)
    sibling = (e + 1 - 2 * core, m)
    partner = (e, 1 - m)
    across = (lax.rem(e + energies // 2, energies), 1 - m)
    z_at = (e // CORES) % ALONG_Z
    way = jnp.where(z_at < ALONG_Z // 2, -1, 1)
    x_next = lax.rem(x_at + way + ALONG_X, ALONG_X)
    x_last = lax.rem(x_at - way + ALONG_X, ALONG_X)
    ring_next = (e + (x_next - x_at) * (CORES * ALONG_Z), m)
    ring_last = (e + (x_last - x_at) * (CORES * ALONG_Z), m)

    load = pltpu.make_async_copy(g_ref.at[0], g_mine, load_sem)
    load.start()
    barrier = pltpu.get_barrier_semaphore()
    greeted = [up, down, sibling, partner, across, ring_next, ring_last]
    for device in greeted:
        pl.semaphore_signal(barrier, inc=1, device_id=device, device_id_type=MESH)
    pl.semaphore_wait(barrier, len(greeted))

    def remote(src, dst, send, recv, device):
        return pltpu.make_async_remote_copy(
            src_ref=src, dst_ref=dst, send_sem=send, recv_sem=recv, device_id=device, device_id_type=MESH
        )

    def at(i, base=0):
        return pl.ds(pl.multiple_of(base + i * CHUNK, CHUNK), CHUNK)

    def rows_at(start):
        return pl.ds(pl.multiple_of(start, CHUNK), CHUNK)

    def to_up(i):
        return remote(x_ref.at[0, at(i)], near.at[0, at(i)], near_send.at[0, i], near_recv.at[0, i], up)

    def to_down(i):
        return remote(x_ref.at[0, at(i)], near.at[1, at(i)], near_send.at[1, i], near_recv.at[1, i], down)

    def to_sibling(i):
        return remote(near.at[1 - core, at(i)], near.at[3, at(i)], fwd_send.at[i], fwd_recv.at[i], sibling)

    def to_partner(k, j):
        return remote(p_out.at[:, j], p_in.at[:, j], p_send.at[k], p_recv.at[k], partner)

    own_to_sibling = remote(x_ref.at[0], near.at[2], sib_send, sib_recv, sibling)

    @pl.loop(0, chunks)
    def _(i):
        to_up(i).start()
        to_down(i).start()

    own_to_sibling.start()

    load.wait()
    half = core * rows
    mine = half + x_at * CHUNK
    g_send_buf[0:CHUNK, :] = g_mine[rows_at(mine), :].astype(F32)
    slice_across = remote(
        g_send_buf.at[pl.ds(0, CHUNK)], g_got.at[rows_at(mine)], g_send.at[0], g_recv.at[0], across
    )
    slice_across.start()
    occ_mine[...] = jnp.full(occ_mine.shape, occ_ref[0, 0].astype(F32), F32)
    occ_copy = remote(occ_mine, occ_got, occ_send, occ_recv, partner)
    occ_copy.start()
    ring_rows = ALONG_X * CHUNK
    direct_rows = rows - ring_rows
    direct = pl.ds(pl.multiple_of(half + ring_rows, CHUNK), direct_rows)
    g_send_buf[CHUNK:, :] = g_mine[direct, :].astype(F32)
    direct_across = remote(
        g_send_buf.at[pl.ds(CHUNK, direct_rows)], g_got.at[direct], g_send.at[1], g_recv.at[1], across
    )
    direct_across.start()

    def prepare(which, matrix):
        @pl.loop(0, norb // LANES)
        def _(i):
            block = pl.ds(pl.multiple_of(i * LANES, LANES), LANES)
            turned[which, :, block] = matrix[block, :].astype(F32).T.astype(BF16)

        own = pl.ds(pl.multiple_of(m * rows, CHUNK), rows)
        cols[which] = turned[which, own, :].astype(F32).T.astype(BF16)

    prepare(0, g_mine)

    occ_copy.wait_recv()
    own_one = off_ref[0] == 1
    own_occ = occ_mine[0:1, 0:1]
    other_occ = occ_got[0:1, 0:1]
    one_sel = jnp.where(own_one, 1.0, 0.0)
    is_one = (one_sel, 1.0 - one_sel)
    low2 = jnp.where(e >= 2, 1.0, 0.0)
    high2 = jnp.where(e < energies - 2, 1.0, 0.0)
    on_core = core.astype(F32)
    third = jnp.where((e > 0) & (e < energies - 1), 1.0, 0.0)
    weights = []
    for occ, one in zip((own_occ, other_occ), is_one):
        weights.append(
            (
                (occ + 1.0) * ((1.0 - one) * low2),
                occ * ((1.0 - one) * high2),
                (occ + on_core) * one,
                (occ + (1.0 - on_core)) * (one * third),
            )
        )

    own_to_sibling.wait_recv()

    def take_chunk(i):
        to_up(i).wait_recv()
        to_down(i).wait_recv()
        to_sibling(i).start()

    def couple(i, which):
        w = weights[which]
        combined = w[0] * near[0, at(i), :] + w[1] * near[1, at(i), :]
        combined = combined + (w[2] * near[2, at(i), :] + w[3] * near[3, at(i), :])
        coupled[which, at(i), :] = dot(combined.astype(BF16), turned[which]).astype(BF16)

    def ring_slice(step, base):
        behind = x_at - way * step + ALONG_X
        return rows_at(base + lax.rem(behind, ALONG_X) * CHUNK)

    def ring_copy(step):
        there = ring_slice(step, half)
        return remote(g_got.at[there], g_got.at[there], g_send.at[2 + step], g_recv.at[2 + step], ring_next)

    def ring_arrival(step):
        there = ring_slice(step, half)
        return remote(
            g_got.at[there], g_got.at[there], g_send.at[1 + step], g_recv.at[1 + step], ring_next
        )

    def share_slice(step, base):
        there = ring_slice(step, base)
        return remote(g_got.at[there], g_got.at[there], g_send.at[5 + step], g_recv.at[5 + step], sibling)

    def share_direct(base):
        there = pl.ds(pl.multiple_of(base + ring_rows, CHUNK), direct_rows)
        return remote(g_got.at[there], g_got.at[there], g_send.at[9], g_recv.at[9], sibling)

    def chunk_step(i):
        take_chunk(i)
        to_sibling(i).wait_recv()
        couple(i, 0)

    def chunk_steps(first, last):
        pl.loop(first, last)(chunk_step)

    chunk_steps(0, 1)
    slice_across.wait_recv()
    ring_copy(0).start()
    share_slice(0, half).start()
    chunk_steps(1, 3)
    ring_arrival(1).wait_recv()
    ring_copy(1).start()
    share_slice(1, half).start()
    chunk_steps(3, 4)
    ring_arrival(2).wait_recv()
    ring_copy(2).start()
    share_slice(2, half).start()
    direct_across.wait_recv()
    share_direct(half).start()
    chunk_steps(4, 5)
    ring_arrival(3).wait_recv()
    share_slice(3, half).start()
    theirs = (1 - core) * rows
    for step in range(ALONG_X):
        share_slice(step, theirs).wait_recv()
    share_direct(theirs).wait_recv()
    prepare(1, g_got)

    @pl.loop(0, 5)
    def _(i):
        couple(i, 1)

    @pl.loop(5, chunks)
    def _(i):
        chunk_step(i)
        couple(i, 1)

    def partial(j, base):
        there = pl.ds(pl.multiple_of(base, CHUNK), rows)
        return dot(cols[0, there, :], coupled[0, :, j]) + dot(cols[1, there, :], coupled[1, :, j])

    pieces = [slice(start, min(start + PIECE, norb)) for start in range(0, norb, PIECE)]
    for k, j in enumerate(pieces):
        p_out[:, j] = partial(j, (1 - m) * rows)
        to_partner(k, j).start()
    for j in pieces:
        o_ref[0, :, j] = partial(j, m * rows) * 0.5
    for k, j in enumerate(pieces):
        to_partner(k, j).wait_recv()
        o_ref[0, :, j] = o_ref[0, :, j] + p_in[:, j] * 0.5
    for k, j in enumerate(pieces):
        to_partner(k, j).wait_send()

    @pl.loop(0, chunks)
    def _(i):
        to_up(i).wait_send()
        to_down(i).wait_send()
        to_sibling(i).wait_send()

    own_to_sibling.wait_send()
    slice_across.wait_send()
    occ_copy.wait_send()
    direct_across.wait_send()
    for step in range(ALONG_X - 1):
        ring_copy(step).wait_send()
    for step in range(ALONG_X):
        share_slice(step, half).wait_send()
    share_direct(half).wait_send()


def shards(energies, spectral, coupling, offsets, occupation):
    _, rows, norb = spectral.shape
    chunks = rows // CHUNK
    dma = pltpu.SemaphoreType.DMA
    anywhere = pl.BlockSpec(memory_space=pltpu.HBM)
    scalar = pl.BlockSpec(memory_space=pltpu.SMEM)
    return pl.pallas_call(
        functools.partial(kernel, energies),
        out_shape=jax.ShapeDtypeStruct(spectral.shape, F32),
        in_specs=[anywhere, anywhere, scalar, scalar],
        out_specs=pl.BlockSpec(memory_space=pltpu.VMEM),
        scratch_shapes=[
            pltpu.VMEM((4, rows, norb), F32),
            pltpu.VMEM((norb, norb), BF16),
            pltpu.VMEM((rows - (ALONG_X - 1) * CHUNK, norb), F32),
            pltpu.VMEM((norb, norb), F32),
            pltpu.VMEM((2, norb, norb), BF16),
            pltpu.VMEM((2, norb, rows), BF16),
            pltpu.VMEM((2, rows, norb), BF16),
            pltpu.VMEM((rows, norb), F32),
            pltpu.VMEM((rows, norb), F32),
            pltpu.VMEM((8, 128), F32),
            pltpu.VMEM((8, 128), F32),
            dma,
            dma((2, chunks)),
            dma((2, chunks)),
            dma((chunks,)),
            dma((chunks,)),
            dma,
            dma,
            dma((10,)),
            dma((10,)),
            dma,
            dma,
            dma((-(-norb // PIECE),)),
            dma((-(-norb // PIECE),)),
        ],
        compiler_params=pltpu.CompilerParams(
            collective_id=0, has_side_effects=True, vmem_limit_bytes=48 << 20
        ),
        name="born_step",
    )(pltpu.with_memory_space_constraint(spectral, pltpu.HBM), pltpu.with_memory_space_constraint(coupling, pltpu.HBM), offsets, occupation)


def solution(mesh):
    return jax.shard_map(
        functools.partial(shards, mesh.shape["energy"]),
        mesh=mesh,
        in_specs=(P("energy", "mode", None), P("mode", None, None), P("mode"), P("mode", "energy")),
        out_specs=P("energy", "mode", None),
        check_vma=False,
    )
```

time: 117 us -> 91.5 us (0.78)
  the two profiles are of different devices: /device:TPU:8 before, /device:TPU:4 now
where the time goes in v2:
time: 91.5 us; the launch traced here: 91.4 us
  Pallas kernels  89 us (97%)
  between operations  1.3 us (1%)
  local copies, waits for them, and re-layouts  1.16 us (1%)
    pallas_call x1, Pallas kernels, shards(): pl.pallas_call(functools.partial(kernel, energies), out_shape=jax.ShapeDt...  89 us

profile of v2, /device:TPU:4, one launch (start us, length us, event | category | flops | bytes accessed | tf_op | source)
XLA Modules:
  0.0 91.4 jit_solution(3235769569725761208)
XLA Ops:
  1.3 89.0 %born_step.1 = f32[1,448,896]{2,1,0:T(8,128)S(1)} custom-call(f32[1,448,896]{2,1,0:T(8,128)} %x_ref.1, bf16[1,896,896]{2,1,0:T(8,128)(2,1)} %g_ref.1, s32[1]{0:T(128)S(6)} %copy.6.off_ref, s32[1,1]{1,0:T(1,128)S(6)} %copy.7.occ_ref), custom_call_target="tpu_custom_call" | custom-call | tf_op jit(solution)/shard_map/born_step/pallas_call | solution.py:278
  90.3 1.2 %copy.8 = f32[1,448,896]{2,1,0:T(8,128)} copy(f32[1,448,896]{2,1,0:T(8,128)S(1)} %born_step.1) | data formatting | bytes 3211264

commit v3 on v2

--- a/solution.py
+++ b/solution.py
@@ -12,6 +12,8 @@
 CHUNK = 64
 LANES = 128
 PIECE = 256
+EARLY = 5
+AHEAD = 5
 F32, BF16 = jnp.float32, jnp.bfloat16
 
 
@@ -57,8 +59,8 @@
     chunks = rows // CHUNK
     core = e % CORES
     x_at = (e // (CORES * ALONG_Z)) % ALONG_X
-    up = (lax.rem(e + 2, energies), m)
-    down = (lax.rem(e + energies - 2, energies), m)
+    first = (lax.rem(e + energies - 2 + 4 * core, energies), m)
+    second = (lax.rem(e + energies + 2 - 4 * core, energies), m)
     sibling = (e + 1 - 2 * core, m)
     partner = (e, 1 - m)
     across = (lax.rem(e + energies // 2, energies), 1 - m)
@@ -72,7 +74,7 @@
     load = pltpu.make_async_copy(g_ref.at[0], g_mine, load_sem)
     load.start()
     barrier = pltpu.get_barrier_semaphore()
-    greeted = [up, down, sibling, partner, across, ring_next, ring_last]
+    greeted = [first, second, sibling, partner, across, ring_next, ring_last]
     for device in greeted:
         pl.semaphore_signal(barrier, inc=1, device_id=device, device_id_type=MESH)
     pl.semaphore_wait(barrier, len(greeted))
@@ -88,14 +90,14 @@
     def rows_at(start):
         return pl.ds(pl.multiple_of(start, CHUNK), CHUNK)
 
-    def to_up(i):
-        return remote(x_ref.at[0, at(i)], near.at[0, at(i)], near_send.at[0, i], near_recv.at[0, i], up)
-
-    def to_down(i):
-        return remote(x_ref.at[0, at(i)], near.at[1, at(i)], near_send.at[1, i], near_recv.at[1, i], down)
+    def to_first(i):
+        return remote(x_ref.at[0, at(i)], near.at[0, at(i)], near_send.at[0, i], near_recv.at[0, i], first)
+
+    def to_second(i):
+        return remote(x_ref.at[0, at(i)], near.at[1, at(i)], near_send.at[1, i], near_recv.at[1, i], second)
 
     def to_sibling(i):
-        return remote(near.at[1 - core, at(i)], near.at[3, at(i)], fwd_send.at[i], fwd_recv.at[i], sibling)
+        return remote(near.at[0, at(i)], near.at[3, at(i)], fwd_send.at[i], fwd_recv.at[i], sibling)
 
     def to_partner(k, j):
         return remote(p_out.at[:, j], p_in.at[:, j], p_send.at[k], p_recv.at[k], partner)
@@ -104,8 +106,7 @@
 
     @pl.loop(0, chunks)
     def _(i):
-        to_up(i).start()
-        to_down(i).start()
+        to_first(i).start()
 
     own_to_sibling.start()
 
@@ -141,38 +142,33 @@
     prepare(0, g_mine)
 
     occ_copy.wait_recv()
-    own_one = off_ref[0] == 1
     own_occ = occ_mine[0:1, 0:1]
     other_occ = occ_got[0:1, 0:1]
-    one_sel = jnp.where(own_one, 1.0, 0.0)
-    is_one = (one_sel, 1.0 - one_sel)
+    own_one = off_ref[0] == 1
+    occ_one = jnp.where(own_one, own_occ, other_occ)
+    occ_two = jnp.where(own_one, other_occ, own_occ)
     low2 = jnp.where(e >= 2, 1.0, 0.0)
     high2 = jnp.where(e < energies - 2, 1.0, 0.0)
     on_core = core.astype(F32)
-    third = jnp.where((e > 0) & (e < energies - 1), 1.0, 0.0)
-    weights = []
-    for occ, one in zip((own_occ, other_occ), is_one):
-        weights.append(
-            (
-                (occ + 1.0) * ((1.0 - one) * low2),
-                occ * ((1.0 - one) * high2),
-                (occ + on_core) * one,
-                (occ + (1.0 - on_core)) * (one * third),
-            )
-        )
+    ends = jnp.where((e > 0) & (e < energies - 1), 1.0, 0.0)
+    which_mode = (jnp.where(own_one, 0, 1), jnp.where(own_one, 1, 0))
+    from_below = (occ_two + 1.0) * low2
+    from_above = occ_two * high2
+    weights = (
+        jnp.where(core == 0, from_above, from_below),
+        jnp.where(core == 0, from_below, from_above),
+        occ_one + on_core,
+        (occ_one + (1.0 - on_core)) * ends,
+    )
 
     own_to_sibling.wait_recv()
 
-    def take_chunk(i):
-        to_up(i).wait_recv()
-        to_down(i).wait_recv()
-        to_sibling(i).start()
-
-    def couple(i, which):
-        w = weights[which]
-        combined = w[0] * near[0, at(i), :] + w[1] * near[1, at(i), :]
-        combined = combined + (w[2] * near[2, at(i), :] + w[3] * near[3, at(i), :])
-        coupled[which, at(i), :] = dot(combined.astype(BF16), turned[which]).astype(BF16)
+    def combine(i, which):
+        a, b = (2, 3) if which == 0 else (0, 1)
+        return (weights[a] * near[a, at(i), :] + weights[b] * near[b, at(i), :]).astype(BF16)
+
+    def couple(there, which, combined):
+        coupled[which, there, :] = dot(combined, turned[which_mode[which]]).astype(BF16)
 
     def ring_slice(step, base):
         behind = x_at - way * step + ALONG_X
@@ -196,29 +192,42 @@
         there = pl.ds(pl.multiple_of(base + ring_rows, CHUNK), direct_rows)
         return remote(g_got.at[there], g_got.at[there], g_send.at[9], g_recv.at[9], sibling)
 
-    def chunk_step(i):
-        take_chunk(i)
-        to_sibling(i).wait_recv()
-        couple(i, 0)
-
-    def chunk_steps(first, last):
-        pl.loop(first, last)(chunk_step)
-
-    chunk_steps(0, 1)
+    def first_steps(start, stop):
+        @pl.loop(start, stop)
+        def _(i):
+            to_first(i).wait_recv()
+            to_sibling(i).start()
+            to_sibling(i).wait_recv()
+            coupled[0, at(i), :] = combine(i, 0)
+
+    def second_step(i):
+        to_second(i).wait_recv()
+        coupled[1, at(i), :] = combine(i, 1)
+
+    def second_steps(start, stop):
+        pl.loop(start, stop)(second_step)
+
+    first_steps(0, 3)
     slice_across.wait_recv()
     ring_copy(0).start()
     share_slice(0, half).start()
-    chunk_steps(1, 3)
+    first_steps(3, 5)
     ring_arrival(1).wait_recv()
     ring_copy(1).start()
     share_slice(1, half).start()
-    chunk_steps(3, 4)
+    first_steps(5, AHEAD)
+
+    @pl.loop(0, chunks)
+    def _(i):
+        to_second(i).start()
+
+    first_steps(AHEAD, chunks)
     ring_arrival(2).wait_recv()
     ring_copy(2).start()
     share_slice(2, half).start()
     direct_across.wait_recv()
     share_direct(half).start()
-    chunk_steps(4, 5)
+    second_steps(0, 2)
     ring_arrival(3).wait_recv()
     share_slice(3, half).start()
     theirs = (1 - core) * rows
@@ -226,21 +235,22 @@
         share_slice(step, theirs).wait_recv()
     share_direct(theirs).wait_recv()
     prepare(1, g_got)
-
-    @pl.loop(0, 5)
-    def _(i):
-        couple(i, 1)
-
-    @pl.loop(5, chunks)
-    def _(i):
-        chunk_step(i)
-        couple(i, 1)
+    couple(pl.ds(0, rows), 0, coupled[0])
+    second_steps(2, EARLY)
+    early = pl.ds(0, EARLY * CHUNK)
+    couple(early, 1, coupled[1, early, :])
+    for i in range(EARLY, chunks):
+        to_second(i).wait_recv()
+        couple(at(i), 1, combine(i, 1))
 
     def partial(j, base):
         there = pl.ds(pl.multiple_of(base, CHUNK), rows)
-        return dot(cols[0, there, :], coupled[0, :, j]) + dot(cols[1, there, :], coupled[1, :, j])
-
-    pieces = [slice(start, min(start + PIECE, norb)) for start in range(0, norb, PIECE)]
+        return dot(cols[which_mode[0], there, :], coupled[0, :, j]) + dot(
+            cols[which_mode[1], there, :], coupled[1, :, j]
+        )
+
+    edges = [0, *range(norb % PIECE, norb + 1, PIECE)]
+    pieces = [slice(a, b) for a, b in zip(edges, edges[1:])]
     for k, j in enumerate(pieces):
         p_out[:, j] = partial(j, (1 - m) * rows)
         to_partner(k, j).start()
@@ -254,8 +264,8 @@
 
     @pl.loop(0, chunks)
     def _(i):
-        to_up(i).wait_send()
-        to_down(i).wait_send()
+        to_first(i).wait_send()
+        to_second(i).wait_send()
         to_sibling(i).wait_send()
 
     own_to_sibling.wait_send()
@@ -273,12 +283,12 @@
     _, rows, norb = spectral.shape
     chunks = rows // CHUNK
     dma = pltpu.SemaphoreType.DMA
-    anywhere = pl.BlockSpec(memory_space=pltpu.HBM)
     scalar = pl.BlockSpec(memory_space=pltpu.SMEM)
+    in_hbm = pl.BlockSpec(memory_space=pltpu.HBM)
     return pl.pallas_call(
         functools.partial(kernel, energies),
         out_shape=jax.ShapeDtypeStruct(spectral.shape, F32),
-        in_specs=[anywhere, anywhere, scalar, scalar],
+        in_specs=[in_hbm, in_hbm, scalar, scalar],
         out_specs=pl.BlockSpec(memory_space=pltpu.VMEM),
         scratch_shapes=[
             pltpu.VMEM((4, rows, norb), F32),
@@ -310,7 +320,7 @@
             collective_id=0, has_side_effects=True, vmem_limit_bytes=48 << 20
         ),
         name="born_step",
-    )(pltpu.with_memory_space_constraint(spectral, pltpu.HBM), pltpu.with_memory_space_constraint(coupling, pltpu.HBM), offsets, occupation)
+    )(*(pltpu.with_memory_space_constraint(a, pltpu.HBM) for a in (spectral, coupling)), offsets, occupation)
 
 
 def solution(mesh):

time: 91.5 us -> 87.1 us (0.952)
  the two profiles are of different devices: /device:TPU:4 before, /device:TPU:8 now
where the time goes in v3:
time: 87.1 us; the launch traced here: 87 us
  Pallas kernels  84.5 us (97%)
  between operations  1.3 us (1%)
  local copies, waits for them, and re-layouts  1.16 us (1%)
    pallas_call x1, Pallas kernels, shards(): pl.pallas_call(functools.partial(kernel, energies), out_shape=jax.ShapeDt...  84.5 us

profile of v3, /device:TPU:8, one launch (start us, length us, event | category | flops | bytes accessed | tf_op | source)
XLA Modules:
  0.0 87.0 jit_solution(12239084817407082074)
XLA Ops:
  1.3 84.5 %born_step.1 = f32[1,448,896]{2,1,0:T(8,128)S(1)} custom-call(f32[1,448,896]{2,1,0:T(8,128)} %x_ref.1, bf16[1,896,896]{2,1,0:T(8,128)(2,1)} %g_ref.1, s32[1]{0:T(128)S(6)} %copy.6.off_ref, s32[1,1]{1,0:T(1,128)S(6)} %copy.7.occ_ref), custom_call_target="tpu_custom_call" | custom-call | tf_op jit(solution)/shard_map/born_step/pallas_call | solution.py:288
  85.8 1.2 %copy.8 = f32[1,448,896]{2,1,0:T(8,128)} copy(f32[1,448,896]{2,1,0:T(8,128)S(1)} %born_step.1) | data formatting | bytes 3211264

commit v4 on v3

--- a/solution.py
+++ b/solution.py
@@ -13,7 +13,7 @@
 LANES = 128
 PIECE = 256
 EARLY = 5
-AHEAD = 5
+SENT = 4
 F32, BF16 = jnp.float32, jnp.bfloat16
 
 
@@ -207,29 +207,29 @@
     def second_steps(start, stop):
         pl.loop(start, stop)(second_step)
 
-    first_steps(0, 3)
     slice_across.wait_recv()
     ring_copy(0).start()
     share_slice(0, half).start()
-    first_steps(3, 5)
+    first_steps(0, 3)
+    to_first(SENT).wait_send()
+
+    @pl.loop(0, chunks)
+    def _(i):
+        to_second(i).start()
+
     ring_arrival(1).wait_recv()
     ring_copy(1).start()
     share_slice(1, half).start()
-    first_steps(5, AHEAD)
-
-    @pl.loop(0, chunks)
-    def _(i):
-        to_second(i).start()
-
-    first_steps(AHEAD, chunks)
+    first_steps(3, 5)
     ring_arrival(2).wait_recv()
     ring_copy(2).start()
     share_slice(2, half).start()
+    first_steps(5, chunks)
     direct_across.wait_recv()
     share_direct(half).start()
-    second_steps(0, 2)
     ring_arrival(3).wait_recv()
     share_slice(3, half).start()
+    second_steps(0, 2)
     theirs = (1 - core) * rows
     for step in range(ALONG_X):
         share_slice(step, theirs).wait_recv()
@@ -264,10 +264,12 @@
 
     @pl.loop(0, chunks)
     def _(i):
-        to_first(i).wait_send()
         to_second(i).wait_send()
         to_sibling(i).wait_send()
 
+    for i in range(chunks):
+        if i != SENT:
+            to_first(i).wait_send()
     own_to_sibling.wait_send()
     slice_across.wait_send()
     occ_copy.wait_send()

time: 87.1 us -> 84.1 us (0.966)
  Pallas kernels: 84.5 us -> 81.5 us
    pallas_call x1, Pallas kernels: 84.5 us -> 81.5 us  [shards(): pl.pallas_call(functools.partial(kernel, energies), out_shape=jax.ShapeDt...]
where the time goes in v4:
time: 84.1 us; the launch traced here: 84 us
  Pallas kernels  81.5 us (97%)
  between operations  1.3 us (2%)
  local copies, waits for them, and re-layouts  1.16 us (1%)
    pallas_call x1, Pallas kernels, shards(): pl.pallas_call(functools.partial(kernel, energies), out_shape=jax.ShapeDt...  81.5 us

profile of v4, /device:TPU:8, one launch (start us, length us, event | category | flops | bytes accessed | tf_op | source)
XLA Modules:
  0.0 84.0 jit_solution(3666003277000637464)
XLA Ops:
  1.3 81.5 %born_step.1 = f32[1,448,896]{2,1,0:T(8,128)S(1)} custom-call(f32[1,448,896]{2,1,0:T(8,128)} %x_ref.1, bf16[1,896,896]{2,1,0:T(8,128)(2,1)} %g_ref.1, s32[1]{0:T(128)S(6)} %copy.6.off_ref, s32[1,1]{1,0:T(1,128)S(6)} %copy.7.occ_ref), custom_call_target="tpu_custom_call" | custom-call | tf_op jit(solution)/shard_map/born_step/pallas_call | solution.py:290
  82.8 1.2 %copy.8 = f32[1,448,896]{2,1,0:T(8,128)} copy(f32[1,448,896]{2,1,0:T(8,128)S(1)} %born_step.1) | data formatting | bytes 3211264

commit v5 on v4

--- a/solution.py
+++ b/solution.py
@@ -74,7 +74,7 @@
     load = pltpu.make_async_copy(g_ref.at[0], g_mine, load_sem)
     load.start()
     barrier = pltpu.get_barrier_semaphore()
-    greeted = [first, second, sibling, partner, across, ring_next, ring_last]
+    greeted = [first, second, sibling, partner, across, ring_last]
     for device in greeted:
         pl.semaphore_signal(barrier, inc=1, device_id=device, device_id_type=MESH)
     pl.semaphore_wait(barrier, len(greeted))
@@ -239,9 +239,12 @@
     second_steps(2, EARLY)
     early = pl.ds(0, EARLY * CHUNK)
     couple(early, 1, coupled[1, early, :])
-    for i in range(EARLY, chunks):
+    for i in range(EARLY, chunks - 1):
         to_second(i).wait_recv()
         couple(at(i), 1, combine(i, 1))
+    last = at(chunks - 1)
+    to_second(chunks - 1).wait_recv()
+    combined = combine(chunks - 1, 1)
 
     def partial(j, base):
         there = pl.ds(pl.multiple_of(base, CHUNK), rows)
@@ -249,9 +252,10 @@
             cols[which_mode[1], there, :], coupled[1, :, j]
         )
 
-    edges = [0, *range(norb % PIECE, norb + 1, PIECE)]
+    edges = [0, 128, 384, 640, 768, 896]
     pieces = [slice(a, b) for a, b in zip(edges, edges[1:])]
     for k, j in enumerate(pieces):
+        coupled[1, last, j] = dot(combined, turned[which_mode[1], :, j]).astype(BF16)
         p_out[:, j] = partial(j, (1 - m) * rows)
         to_partner(k, j).start()
     for j in pieces:
@@ -315,8 +319,8 @@
             dma((10,)),
             dma,
             dma,
-            dma((-(-norb // PIECE),)),
-            dma((-(-norb // PIECE),)),
+            dma((5,)),
+            dma((5,)),
         ],
         compiler_params=pltpu.CompilerParams(
             collective_id=0, has_side_effects=True, vmem_limit_bytes=48 << 20

time: 84.1 us -> 84.1 us (level)
  no operation moved by 1% of the time
where the time goes in v5:
time: 84.1 us; the launch traced here: 83.9 us
  Pallas kernels  81.5 us (97%)
  between operations  1.3 us (2%)
  local copies, waits for them, and re-layouts  1.16 us (1%)
    pallas_call x1, Pallas kernels, shards(): pl.pallas_call(functools.partial(kernel, energies), out_shape=jax.ShapeDt...  81.5 us

profile of v5, /device:TPU:8, one launch (start us, length us, event | category | flops | bytes accessed | tf_op | source)
XLA Modules:
  0.0 83.9 jit_solution(6092661816637525310)
XLA Ops:
  1.3 81.5 %born_step.1 = f32[1,448,896]{2,1,0:T(8,128)S(1)} custom-call(f32[1,448,896]{2,1,0:T(8,128)} %x_ref.1, bf16[1,896,896]{2,1,0:T(8,128)(2,1)} %g_ref.1, s32[1]{0:T(128)S(6)} %copy.6.off_ref, s32[1,1]{1,0:T(1,128)S(6)} %copy.7.occ_ref), custom_call_target="tpu_custom_call" | custom-call | tf_op jit(solution)/shard_map/born_step/pallas_call | solution.py:294
  82.8 1.2 %copy.8 = f32[1,448,896]{2,1,0:T(8,128)} copy(f32[1,448,896]{2,1,0:T(8,128)S(1)} %born_step.1) | data formatting | bytes 3211264

commit v6 on v5

--- a/solution.py
+++ b/solution.py
@@ -260,12 +260,6 @@
         to_partner(k, j).start()
     for j in pieces:
         o_ref[0, :, j] = partial(j, m * rows) * 0.5
-    for k, j in enumerate(pieces):
-        to_partner(k, j).wait_recv()
-        o_ref[0, :, j] = o_ref[0, :, j] + p_in[:, j] * 0.5
-    for k, j in enumerate(pieces):
-        to_partner(k, j).wait_send()
-
     @pl.loop(0, chunks)
     def _(i):
         to_second(i).wait_send()
@@ -283,6 +277,11 @@
     for step in range(ALONG_X):
         share_slice(step, half).wait_send()
     share_direct(half).wait_send()
+
+    for k, j in enumerate(pieces):
+        to_partner(k, j).wait_send()
+        to_partner(k, j).wait_recv()
+        o_ref[0, :, j] = o_ref[0, :, j] + p_in[:, j] * 0.5
 
 
 def shards(energies, spectral, coupling, offsets, occupation):

time: 84.1 us -> 84 us (level)
  no operation moved by 1% of the time
where the time goes in v6:
time: 84 us; the launch traced here: 83.9 us
  Pallas kernels  81.4 us (97%)
  between operations  1.3 us (2%)
  local copies, waits for them, and re-layouts  1.16 us (1%)
    pallas_call x1, Pallas kernels, shards(): pl.pallas_call(functools.partial(kernel, energies), out_shape=jax.ShapeDt...  81.4 us

profile of v6, /device:TPU:8, one launch (start us, length us, event | category | flops | bytes accessed | tf_op | source)
XLA Modules:
  0.0 83.9 jit_solution(6409488722507856247)
XLA Ops:
  1.3 81.4 %born_step.1 = f32[1,448,896]{2,1,0:T(8,128)S(1)} custom-call(f32[1,448,896]{2,1,0:T(8,128)} %x_ref.1, bf16[1,896,896]{2,1,0:T(8,128)(2,1)} %g_ref.1, s32[1]{0:T(128)S(6)} %copy.6.off_ref, s32[1,1]{1,0:T(1,128)S(6)} %copy.7.occ_ref), custom_call_target="tpu_custom_call" | custom-call | tf_op jit(solution)/shard_map/born_step/pallas_call | solution.py:293
  82.7 1.2 %copy.8 = f32[1,448,896]{2,1,0:T(8,128)} copy(f32[1,448,896]{2,1,0:T(8,128)S(1)} %born_step.1) | data formatting | bytes 3211264

commit v7 on v6

--- a/solution.py
+++ b/solution.py
@@ -13,7 +13,7 @@
 LANES = 128
 PIECE = 256
 EARLY = 5
-SENT = 4
+SENT = 3
 F32, BF16 = jnp.float32, jnp.bfloat16
 
 

time: 84 us -> 84 us (level)
  no operation moved by 1% of the time
where the time goes in v7:
time: 84 us; the launch traced here: 83.9 us
  Pallas kernels  81.4 us (97%)
  between operations  1.3 us (2%)
  local copies, waits for them, and re-layouts  1.16 us (1%)
    pallas_call x1, Pallas kernels, shards(): pl.pallas_call(functools.partial(kernel, energies), out_shape=jax.ShapeDt...  81.4 us

profile of v7, /device:TPU:8, one launch (start us, length us, event | category | flops | bytes accessed | tf_op | source)
XLA Modules:
  0.0 83.9 jit_solution(15614804930143718398)
XLA Ops:
  1.3 81.4 %born_step.1 = f32[1,448,896]{2,1,0:T(8,128)S(1)} custom-call(f32[1,448,896]{2,1,0:T(8,128)} %x_ref.1, bf16[1,896,896]{2,1,0:T(8,128)(2,1)} %g_ref.1, s32[1]{0:T(128)S(6)} %copy.6.off_ref, s32[1,1]{1,0:T(1,128)S(6)} %copy.7.occ_ref), custom_call_target="tpu_custom_call" | custom-call | tf_op jit(solution)/shard_map/born_step/pallas_call | solution.py:293
  82.7 1.2 %copy.8 = f32[1,448,896]{2,1,0:T(8,128)} copy(f32[1,448,896]{2,1,0:T(8,128)S(1)} %born_step.1) | data formatting | bytes 3211264
